TPU v7x, 128 devices: a whole 4x4x4 slice. The times are simulated.
128 devices in a mesh: row: 16 (over x, y_hi, core), col: 8 (over z, y_lo).
Axes of the slice: x: 4, y: 4 (y_hi: 2, y_lo: 2; y = y_hi * 2 + y_lo), z: 4, core: 2. Of those that a mesh axis runs over, the one named last changes fastest.
Arguments:
- counts: int32 [16384, 16384], P('row', 'col'), may hold values from 0 to 33, as said below
- row_emb: float32 [256, 16384], P('col', 'row'), may hold values from -2 to 2
- col_emb: float32 [256, 16384], P('row', 'col'), may hold values from -2 to 2
- row_accum: float32 [256, 16384], P('col', 'row'), may hold values from 100 to 10000
- col_accum: float32 [256, 16384], P('row', 'col'), may hold values from 100 to 10000
Outputs:
- new_row_emb: float32 [256, 16384], P('col', 'row')
- new_col_emb: float32 [256, 16384], P('row', 'col')
Inputs may be any that keep to these rules, and one draw needn't show every extreme that they name: `counts`: every row word and every column word has a positive count with some partner.
All inputs are finite; a program needn't handle non-finite values.
Results may differ from a plain program's by a relative error of at most 0.0015.
Values may be sent and summed in bfloat16 or wider, within the bound.
No kernel may reach another device: no remote copies, remote signals or barrier semaphores. Data moves between devices by JAX's collectives and lax.ppermute only.
A program may use at most 64 MiB of HBM per device.

v0:
```python
import jax
import jax.numpy as jnp
from jax import lax
from jax.sharding import PartitionSpec as P

SWEEPS = 2


def copy_for_each(value, axis):
    length = lax.axis_size(axis)
    return lax.all_to_all(
        jnp.broadcast_to(value[None], (length, *value.shape)), axis, 0, 0, tiled=True
    )


def in_order(tiles, dim):
    tiles = jnp.moveaxis(tiles, 0, dim)
    lengths = tiles.shape
    return tiles.reshape(*lengths[:dim], lengths[dim] * lengths[dim + 1], *lengths[dim + 2 :])


def gathered_copies(value, axis, dim):
    tiles = copy_for_each(value, axis)
    return in_order(tiles, dim)


def split_up(value, dim, length):
    before, after = (value.shape[:dim], value.shape[dim + 1 :])
    return jnp.moveaxis(value.reshape(*before, length, -1, *after), dim, 0)


def sent_and_summed(value, axis, dim):
    tiles = split_up(value, dim, lax.axis_size(axis))
    arrived = lax.all_to_all(tiles, axis, split_axis=0, concat_axis=0, tiled=True)
    return arrived.astype(jnp.float32).sum(axis=0)


def over_copies(value, axis):
    everything = copy_for_each(value, axis)
    return jnp.sum(everything, axis=0)


def sweep_once(row_emb, col_emb, row_accum, col_accum, positive, target, weight):
    row_half = row_emb.astype(jnp.bfloat16)
    col_half = col_emb.astype(jnp.bfloat16)
    row_block = gathered_copies(row_half, "col", 0)
    col_block = lax.all_gather(col_half, "row", axis=0, tiled=True)
    scores = lax.dot_general(
        row_block, col_block, (((0,), (0,)), ((), ())), preferred_element_type=jnp.float32
    )
    errors = scores - target
    grads = jnp.where(positive, weight * errors, jax.nn.sigmoid(errors)).astype(jnp.bfloat16)
    piece = col_block
    row_grad = sent_and_summed(
        lax.dot_general(
            piece, grads, (((1,), (1,)), ((), ())), preferred_element_type=jnp.float32
        ).astype(jnp.bfloat16),
        "col",
        0,
    )
    piece = row_block
    col_grad = sent_and_summed(
        jnp.dot(piece, grads, preferred_element_type=jnp.float32).astype(jnp.bfloat16), "row", 0
    )
    row_accum = row_accum + row_grad * row_grad
    row_emb = row_emb - 0.05 * row_grad / jnp.sqrt(row_accum)
    col_accum = col_accum + col_grad * col_grad
    col_emb = col_emb - 0.05 * col_grad / jnp.sqrt(col_accum)
    return (row_emb, col_emb, row_accum, col_accum)


def on_device(counts, row_emb, col_emb, row_accum, col_accum):
    values = counts.astype(jnp.float32)
    local_rows = jnp.sum(values, axis=1)
    local_cols = jnp.sum(values, axis=0)
    row_marg = over_copies(local_rows, "col")
    col_marg = over_copies(local_cols, "row")
    total = over_copies(jnp.sum(row_marg), "row")
    target = (
        jnp.log(jnp.maximum(values, 1.0))
        + jnp.log(total)
        - jnp.log(row_marg)[:, None]
        - jnp.log(col_marg)[None, :]
    )
    weight = 0.1 + 0.25 * jnp.sqrt(values)
    positive = counts > 0
    for sweep in range(SWEEPS):
        row_emb, col_emb, row_accum, col_accum = sweep_once(
            row_emb, col_emb, row_accum, col_accum, positive, target, weight
        )
    return (row_emb, col_emb)


def solution(mesh):
    in_specs = (P("row", "col"), P("col", "row"), P("row", "col"), P("col", "row"), P("row", "col"))
    out_specs = (P("col", "row"), P("row", "col"))
    return jax.shard_map(
        on_device, mesh=mesh, in_specs=in_specs, out_specs=out_specs, check_vma=False
    )
```

profile of v0, /device:TPU:1, one launch (start us, length us, event | category | flops | bytes accessed | tf_op | source)
XLA Modules:
  0.0 206.4 jit_solution(5882931983976948135)
XLA Ops:
  7.2 1.6 convert_element_type.53
  8.8 4.6 %convert_reduce_fusion.1 = (f32[1024]{0:T(1024)S(1)}, f32[2048]{0:T(1024)S(1)}) fusion(s32[1024,2048]{1,0:T(8,128)} %param.5), kind=kLoop, calls=%fused_computation.5 | loop fusion | flops 6288384 | bytes 8400896 | tf_op jit(solution)/shard_map/reduce_sum | solution.py:74
  13.5 11.8 %all_to_all.48 = f32[8,1,1024]{2,1,0:T(1,128)S(1)} all-to-all(f32[8,1,1024]{2,1,0:T(1,128)S(1)} %broadcast_in_dim.11), channel_id=1, replica_groups=mesh['row'=16,'col'=8] {'col'}, dimensions={0} | all-to-all | bytes 65536 | tf_op jit(solution)/shard_map/all_to_all | solution.py:11
  25.3 0.7 fusion.2
  25.9 0.6 broadcast_in_dim.12
  26.6 15.6 %all_to_all.49 = f32[16,1,1]{2,1,0:T(1,128)S(1)} all-to-all(f32[16,1,1]{2,1,0:T(1,128)S(1)} %broadcast_in_dim.12), channel_id=1, replica_groups=mesh['row'=16,'col'=8] {'row'}, dimensions={0} | all-to-all | bytes 128 | tf_op jit(solution)/shard_map/all_to_all | solution.py:11
  42.1 0.7 broadcast_in_dim.13
  42.9 4.0 %all-to-all-start.3 = ((f32[16,1,2048]{2,1,0:T(1,128)}), f32[16,1,2048]{2,1,0:T(1,128)S(1)}, u32[]{:S(2)}, u32[]{:S(2)}) async-start(f32[16,1,2048]{2,1,0:T(1,128)} %broadcast_in_dim.13), calls=%async_computation.3 | async-start | bytes 262144 | tf_op jit(solution)/shard_map/all_to_all | solution.py:11
  46.9 8.2 %all-to-all-done.3 = f32[16,1,2048]{2,1,0:T(1,128)S(1)} async-done(((f32[16,1,2048]{2,1,0:T(1,128)}), f32[16,1,2048]{2,1,0:T(1,128)S(1)}, u32[]{:S(2)}, u32[]{:S(2)}) %all-to-all-start.3) | async-done | bytes 131104 | tf_op jit(solution)/shard_map/all_to_all | solution.py:11
  55.1 0.8 broadcast_in_dim.10
  55.9 3.5 %all-to-all-start = ((bf16[8,32,1024]{2,1,0:T(8,128)(2,1)}), bf16[8,32,1024]{2,1,0:T(8,128)(2,1)S(1)}, u32[]{:S(2)}, u32[]{:S(2)}) async-start(bf16[8,32,1024]{2,1,0:T(8,128)(2,1)} %broadcast_in_dim.10), calls=%async_computation | async-start | bytes 1048576 | tf_op jit(solution)/shard_map/all_to_all | solution.py:11
  59.5 0.6 reduce_sum.92
  60.9 8.0 %all-to-all-done = bf16[8,32,1024]{2,1,0:T(8,128)(2,1)S(1)} async-done(((bf16[8,32,1024]{2,1,0:T(8,128)(2,1)}), bf16[8,32,1024]{2,1,0:T(8,128)(2,1)S(1)}, u32[]{:S(2)}, u32[]{:S(2)}) %all-to-all-start) | async-done | bytes 524320 | tf_op jit(solution)/shard_map/all_to_all | solution.py:11
  68.9 12.8 %select_convert_fusion.1 = bf16[1024,2048]{1,0:T(8,128)(2,1)S(1)} fusion(s32[1024,2048]{1,0:T(8,128)} %param.5, bf16[256,1024]{1,0:T(8,128)(2,1)S(1)} %bitcast.23, bf16[256,2048]{1,0:T(8,128)(2,1)} %all-gather.3.cloned.1.call-done, f32[2048]{0:T(1024)S(1)} %log.23, f32[1024]{0:T(1024)S(1)} %log.22, f32[]{:T(128)S(6)} %log.21), kind=kOutput, calls=%fused_computation.1 | convolution fusion | flops 1105199104 | bytes 14168068 | tf_op jit(solution)/shard_map/dot_general | solution.py:48
  81.8 1.3 convolution_convert_fusion
  83.1 21.2 %all_to_all.50 = bf16[16,16,2048]{2,1,0:T(8,128)(2,1)S(1)} all-to-all(bf16[16,16,2048]{2,1,0:T(8,128)(2,1)S(1)} %bitcast.22), channel_id=1, replica_groups=mesh['row'=16,'col'=8] {'row'}, dimensions={0} | all-to-all | bytes 2097152 | tf_op jit(solution)/shard_map/all_to_all | solution.py:34
  104.3 0.1 convert_reduce_fusion.3
  104.4 0.7 fusion.1
  105.1 3.5 %convolution_convert_fusion.3 = bf16[1024,256]{0,1:T(8,128)(2,1)S(1)} fusion(bf16[1024,2048]{1,0:T(8,128)(2,1)} %copy-done.6, bf16[256,2048]{1,0:T(8,128)(2,1)S(1)} %copy-done.4), kind=kOutput, calls=%fused_computation.12 | convolution fusion | flops 1074003968 | bytes 5767168 | tf_op jit(solution)/shard_map/dot_general | solution.py:55
  108.6 12.2 %all_to_all.51 = bf16[8,32,1024]{2,1,0:T(8,128)(2,1)S(1)} all-to-all(bf16[8,32,1024]{2,1,0:T(8,128)(2,1)S(1)} %bitcast.27), channel_id=1, replica_groups=mesh['row'=16,'col'=8] {'col'}, dimensions={0} | all-to-all | bytes 1048576 | tf_op jit(solution)/shard_map/all_to_all | solution.py:34
  121.0 10.8 %all_to_all.52 = bf16[8,32,1024]{2,1,0:T(8,128)(2,1)S(1)} all-to-all(bf16[8,32,1024]{2,1,0:T(8,128)(2,1)S(1)} %broadcast_in_dim.14), channel_id=1, replica_groups=mesh['row'=16,'col'=8] {'col'}, dimensions={0} | all-to-all | bytes 1048576 | tf_op jit(solution)/shard_map/all_to_all | solution.py:11
  131.8 14.3 %all-gather.5.cloned.1.call-done = bf16[256,2048]{1,0:T(8,128)(2,1)} async-done(((bf16[16,2048]{1,0:T(8,128)(2,1)}), bf16[256,2048]{1,0:T(8,128)(2,1)}) %all-gather.5.cloned.1.call-update) | async-done | bytes 1048592 | tf_op jit(solution)/shard_map/all_gather | solution.py:47
  146.1 13.2 %select_convert_fusion = bf16[1024,2048]{1,0:T(8,128)(2,1)S(1)} fusion(s32[1024,2048]{1,0:T(8,128)} %param.5, bf16[256,1024]{1,0:T(8,128)(2,1)S(1)} %bitcast.25, bf16[256,2048]{1,0:T(8,128)(2,1)} %all-gather.5.cloned.1.call-done, f32[2048]{0:T(1024)S(1)} %log.23, f32[1024]{0:T(1024)S(1)} %log.22, f32[]{:T(128)S(6)} %log.21), kind=kOutput, calls=%fused_computation | convolution fusion | flops 1105199104 | bytes 14168068 | tf_op jit(solution)/shard_map/dot_general | solution.py:48
  159.4 2.1 %convolution_convert_fusion.2 = bf16[256,1024]{1,0:T(8,128)(2,1)} fusion(bf16[256,2048]{1,0:T(8,128)(2,1)S(1)} %copy-done.5, bf16[1024,2048]{1,0:T(8,128)(2,1)S(1)} %select_convert_fusion), kind=kOutput, calls=%fused_computation.11 | convolution fusion | flops 1074003968 | bytes 5767168 | tf_op jit(solution)/shard_map/dot_general | solution.py:55
  161.5 4.2 %all-to-all-start.7 = ((bf16[8,32,1024]{2,1,0:T(8,128)(2,1)}), bf16[8,32,1024]{2,1,0:T(8,128)(2,1)S(1)}, u32[]{:S(2)}, u32[]{:S(2)}) async-start(bf16[8,32,1024]{2,1,0:T(8,128)(2,1)} %bitcast.6), calls=%async_computation.7 | async-start | bytes 1048576 | tf_op jit(solution)/shard_map/all_to_all | solution.py:34
  165.6 4.4 %convolution_convert_fusion.1 = bf16[256,2048]{1,0:T(8,128)(2,1)} fusion(bf16[256,1024]{1,0:T(8,128)(2,1)S(1)} %bitcast.26, bf16[1024,2048]{1,0:T(8,128)(2,1)} %copy-done.7), kind=kOutput, calls=%fused_computation.8 | convolution fusion | flops 1074266112 | bytes 5767168 | tf_op jit(solution)/shard_map/dot_general | solution.py:63
  170.1 4.9 %all-to-all-done.7 = bf16[8,32,1024]{2,1,0:T(8,128)(2,1)S(1)} async-done(((bf16[8,32,1024]{2,1,0:T(8,128)(2,1)}), bf16[8,32,1024]{2,1,0:T(8,128)(2,1)S(1)}, u32[]{:S(2)}, u32[]{:S(2)}) %all-to-all-start.7) | async-done | bytes 524320 | tf_op jit(solution)/shard_map/all_to_all | solution.py:34
  175.0 6.8 %all-to-all-start.8 = ((bf16[16,16,2048]{2,1,0:T(8,128)(2,1)}), bf16[16,16,2048]{2,1,0:T(8,128)(2,1)S(1)}, u32[]{:S(2)}, u32[]{:S(2)}) async-start(bf16[16,16,2048]{2,1,0:T(8,128)(2,1)} %bitcast.7), calls=%async_computation.8 | async-start | bytes 2097152 | tf_op jit(solution)/shard_map/all_to_all | solution.py:34
  181.9 0.7 multiply_subtract_fusion.1
  182.6 16.1 %all-to-all-done.8 = bf16[16,16,2048]{2,1,0:T(8,128)(2,1)S(1)} async-done(((bf16[16,16,2048]{2,1,0:T(8,128)(2,1)}), bf16[16,16,2048]{2,1,0:T(8,128)(2,1)S(1)}, u32[]{:S(2)}, u32[]{:S(2)}) %all-to-all-start.8) | async-done | bytes 1048608 | tf_op jit(solution)/shard_map/all_to_all | solution.py:34
  198.7 0.1 convert_reduce_fusion.2
  198.9 0.7 multiply_subtract_fusion
  (30 shorter events, 0.5 us)
Async XLA Ops:
  7.2 39.7 %copy-start = (f32[32,1024]{1,0:T(8,128)S(1)}, f32[32,1024]{1,0:T(8,128)}, u32[]{:S(2)}) copy-start(f32[32,1024]{1,0:T(8,128)} %param.6) | copy-start | bytes 393220
  7.2 61.8 %all-gather.3.cloned.1.call-start = ((), (), s32[]{:S(2)}) async-start(), calls=%async_computation.9 | async-start | bytes 1114112 | tf_op jit(solution)/shard_map/all_gather | solution.py:47
  42.9 12.2 %all-to-all-start.3 = ((f32[16,1,2048]{2,1,0:T(1,128)}), f32[16,1,2048]{2,1,0:T(1,128)S(1)}, u32[]{:S(2)}, u32[]{:S(2)}) async-start(f32[16,1,2048]{2,1,0:T(1,128)} %broadcast_in_dim.13), calls=%async_computation.3 | async-start | bytes 262144 | tf_op jit(solution)/shard_map/all_to_all | solution.py:11
  55.9 13.0 %all-to-all-start = ((bf16[8,32,1024]{2,1,0:T(8,128)(2,1)}), bf16[8,32,1024]{2,1,0:T(8,128)(2,1)S(1)}, u32[]{:S(2)}, u32[]{:S(2)}) async-start(bf16[8,32,1024]{2,1,0:T(8,128)(2,1)} %broadcast_in_dim.10), calls=%async_computation | async-start | bytes 1048576 | tf_op jit(solution)/shard_map/all_to_all | solution.py:11
  59.4 86.7 %all-gather.5.cloned.1.call-start = ((), (), s32[]{:S(2)}) async-start(), calls=%async_computation.10 | async-start | bytes 1114112 | tf_op jit(solution)/shard_map/all_gather | solution.py:47
  81.8 22.6 %copy-start.6 = (bf16[1024,2048]{1,0:T(8,128)(2,1)}, bf16[1024,2048]{1,0:T(8,128)(2,1)S(1)}, u32[]{:S(2)}) copy-start(bf16[1024,2048]{1,0:T(8,128)(2,1)S(1)} %select_convert_fusion.1) | copy-start | bytes 12582916
  81.8 22.6 %copy-start.1 = (f32[16,2048]{1,0:T(8,128)S(1)}, f32[16,2048]{1,0:T(8,128)}, u32[]{:S(2)}) copy-start(f32[16,2048]{1,0:T(8,128)} %param.7) | copy-start | bytes 393220
  81.8 22.6 %copy-start.3 = (f32[16,2048]{1,0:T(8,128)S(1)}, f32[16,2048]{1,0:T(8,128)}, u32[]{:S(2)}) copy-start(f32[16,2048]{1,0:T(8,128)} %param.9) | copy-start | bytes 393220
  81.8 23.3 %copy-start.4 = (bf16[256,2048]{1,0:T(8,128)(2,1)S(1)}, bf16[256,2048]{1,0:T(8,128)(2,1)}, u32[]{:S(2)}) copy-start(bf16[256,2048]{1,0:T(8,128)(2,1)} %all-gather.3.cloned.1.call-done) | copy-start | bytes 3145732
  81.8 39.1 %copy-start.2 = (f32[32,1024]{1,0:T(8,128)S(1)}, f32[32,1024]{1,0:T(8,128)}, u32[]{:S(2)}) copy-start(f32[32,1024]{1,0:T(8,128)} %param.8) | copy-start | bytes 393220
  146.1 13.2 %copy-start.5 = (bf16[256,2048]{1,0:T(8,128)(2,1)S(1)}, bf16[256,2048]{1,0:T(8,128)(2,1)}, u32[]{:S(2)}) copy-start(bf16[256,2048]{1,0:T(8,128)(2,1)} %all-gather.5.cloned.1.call-done) | copy-start | bytes 3145732
  159.4 2.1 %copy-start.7 = (bf16[1024,2048]{1,0:T(8,128)(2,1)}, bf16[1024,2048]{1,0:T(8,128)(2,1)S(1)}, u32[]{:S(2)}) copy-start(bf16[1024,2048]{1,0:T(8,128)(2,1)S(1)} %select_convert_fusion) | copy-start | bytes 12582916
  161.5 13.5 %all-to-all-start.7 = ((bf16[8,32,1024]{2,1,0:T(8,128)(2,1)}), bf16[8,32,1024]{2,1,0:T(8,128)(2,1)S(1)}, u32[]{:S(2)}, u32[]{:S(2)}) async-start(bf16[8,32,1024]{2,1,0:T(8,128)(2,1)} %bitcast.6), calls=%async_computation.7 | async-start | bytes 1048576 | tf_op jit(solution)/shard_map/all_to_all | solution.py:34
  175.0 23.8 %all-to-all-start.8 = ((bf16[16,16,2048]{2,1,0:T(8,128)(2,1)}), bf16[16,16,2048]{2,1,0:T(8,128)(2,1)S(1)}, u32[]{:S(2)}, u32[]{:S(2)}) async-start(bf16[16,16,2048]{2,1,0:T(8,128)(2,1)} %bitcast.7), calls=%async_computation.8 | async-start | bytes 2097152 | tf_op jit(solution)/shard_map/all_to_all | solution.py:34
Sparse Core Ops, SparseCore 0:
  10.9 48.3 all-gather.2
  105.2 40.8 all-gather.4
where the time goes:
time: 207 us; the launch traced here: 206 us
  blocking collectives  71.5 us (35%)
  waiting for transfers between devices  51.6 us (25%)
  matrix products  37.3 us (18%)
  starting transfers between devices  18.5 us (9%)
  between operations  15 us (7%)
  other arithmetic  10.2 us (5%)
  local copies, waits for them, and re-layouts  2.34 us (1%)
    all_to_all x3, blocking collectives, copy_for_each(): lax.all_to_all(jnp.broadcast_to(value[None], (length, *value.shape)), axi...  38.1 us
    all_to_all x2, blocking collectives, sent_and_summed(): lax.all_to_all(tiles, axis, split_axis=0, concat_axis=0, tiled=True)  33.3 us
    dot_general x2, matrix products, sweep_once(): lax.dot_general(row_block, col_block, (((0,), (0,)), ((), ())), preferred...  26.1 us
    all_to_all x2, waiting for transfers between devices, sent_and_summed(): lax.all_to_all(tiles, axis, split_axis=0, concat_axis=0, tiled=True)  21 us
    all_to_all x2, waiting for transfers between devices, copy_for_each(): lax.all_to_all(jnp.broadcast_to(value[None], (length, *value.shape)), axi...  16.2 us
    all_gather x2, waiting for transfers between devices, sweep_once(): col_block = lax.all_gather(col_half, 'row', axis=0, tiled=True)  14.3 us
    all_to_all x2, starting transfers between devices, sent_and_summed(): lax.all_to_all(tiles, axis, split_axis=0, concat_axis=0, tiled=True)  11 us
    all_to_all x2, starting transfers between devices, copy_for_each(): lax.all_to_all(jnp.broadcast_to(value[None], (length, *value.shape)), axi...  7.46 us
  transfers between devices with their start and end apart: 6, of which 5 were waited for; matrix products, arithmetic and copies ran while one was open for 8% of the time, Pallas kernels for 0%

commit v1 on v0

--- a/solution.py
+++ b/solution.py
@@ -2,8 +2,16 @@
 import jax.numpy as jnp
 from jax import lax
 from jax.sharding import PartitionSpec as P
+from jax.lax import all_to_all, axis_size
 
 SWEEPS = 2
+
+
+def positions_draft(shard_in, bus_axis):
+    step_out = jnp.stack([shard_in for _ in range(axis_size(bus_axis))])
+    b_now = all_to_all(step_out, split_axis=0, concat_axis=0, axis_name=bus_axis)
+    high = jnp.concatenate(b_now, 0)
+    return high
 
 
 def copy_for_each(value, axis):
@@ -44,7 +52,7 @@
     row_half = row_emb.astype(jnp.bfloat16)
     col_half = col_emb.astype(jnp.bfloat16)
     row_block = gathered_copies(row_half, "col", 0)
-    col_block = lax.all_gather(col_half, "row", axis=0, tiled=True)
+    col_block = positions_draft(col_half, "row")
     scores = lax.dot_general(
         row_block, col_block, (((0,), (0,)), ((), ())), preferred_element_type=jnp.float32
     )

time: 207 us -> 222 us (1.072)
  waiting for transfers between devices: 51.6 us -> 83.6 us
  blocking collectives: 71.5 us -> 50 us
  starting transfers between devices: 18.5 us -> 34.4 us
  between operations: 15 us -> 1.53 us
    all_to_all x2 -> x4, waiting for transfers between devices: 21 us -> 42.2 us  [sent_and_summed(): lax.all_to_all(tiles, axis, split_axis=0, concat_axis=0, tiled=True)]
    all_to_all x0 -> x1, waiting for transfers between devices: none -> 15.6 us  [positions_draft(): all_to_all(step_out, split_axis=0, concat_axis=0, axis_name=bus_axis)]
    all_gather x2 -> x0, waiting for transfers between devices: 14.3 us -> none  [sweep_once(): col_block = lax.all_gather(col_half, 'row', axis=0, tiled=True)]
    all_to_all x3 -> x2, blocking collectives: 38.1 us -> 27.3 us  [copy_for_each(): lax.all_to_all(jnp.broadcast_to(value[None], (length, *value.shape)), axi...]
    all_to_all x2 -> x1, blocking collectives: 33.3 us -> 22.6 us  [positions_draft(): all_to_all(step_out, split_axis=0, concat_axis=0, axis_name=bus_axis)]
    all_to_all x2 -> x3, waiting for transfers between devices: 16.2 us -> 25.8 us  [copy_for_each(): lax.all_to_all(jnp.broadcast_to(value[None], (length, *value.shape)), axi...]
    all_to_all x2 -> x4, starting transfers between devices: 11 us -> 18.4 us  [sent_and_summed(): lax.all_to_all(tiles, axis, split_axis=0, concat_axis=0, tiled=True)]
    all_to_all x0 -> x1, starting transfers between devices: none -> 5.06 us  [positions_draft(): all_to_all(step_out, split_axis=0, concat_axis=0, axis_name=bus_axis)]
  transfers between devices with their start and end apart: 6 -> 8, of which waited for: 5 -> 8; matrix products, arithmetic and copies ran while one was open for 8% -> 5% of each run, Pallas kernels for 0% -> 0%
where the time goes in v1:
time: 222 us; the launch traced here: 221 us
  waiting for transfers between devices  83.6 us (38%)
  blocking collectives  50 us (23%)
  matrix products  38.8 us (17%)
  starting transfers between devices  34.4 us (15%)
  other arithmetic  8.05 us (4%)
  local copies, waits for them, and re-layouts  4.34 us (2%)
    all_to_all x4, waiting for transfers between devices, sent_and_summed(): lax.all_to_all(tiles, axis, split_axis=0, concat_axis=0, tiled=True)  42.2 us
    all_to_all x2, blocking collectives, copy_for_each(): lax.all_to_all(jnp.broadcast_to(value[None], (length, *value.shape)), axi...  27.3 us
    all_to_all x3, waiting for transfers between devices, copy_for_each(): lax.all_to_all(jnp.broadcast_to(value[None], (length, *value.shape)), axi...  25.8 us
    dot_general x2, matrix products, sweep_once(): lax.dot_general(row_block, col_block, (((0,), (0,)), ((), ())), preferred...  25.7 us
    all_to_all x1, blocking collectives, positions_draft(): all_to_all(step_out, split_axis=0, concat_axis=0, axis_name=bus_axis)  22.6 us
    all_to_all x4, starting transfers between devices, sent_and_summed(): lax.all_to_all(tiles, axis, split_axis=0, concat_axis=0, tiled=True)  18.4 us
    all_to_all x1, waiting for transfers between devices, positions_draft(): all_to_all(step_out, split_axis=0, concat_axis=0, axis_name=bus_axis)  15.6 us
    all_to_all x3, starting transfers between devices, copy_for_each(): lax.all_to_all(jnp.broadcast_to(value[None], (length, *value.shape)), axi...  11 us
  transfers between devices with their start and end apart: 8, of which 8 were waited for; matrix products, arithmetic and copies ran while one was open for 5% of the time, Pallas kernels for 0%

profile of v1, /device:TPU:1, one launch (start us, length us, event | category | flops | bytes accessed | tf_op | source)
XLA Modules:
  0.0 220.7 jit_solution(15094790278284111871)
XLA Ops:
  0.6 4.7 %convert_reduce_fusion.1 = (f32[1024]{0:T(1024)S(1)}, f32[2048]{0:T(1024)S(1)}) fusion(s32[1024,2048]{1,0:T(8,128)} %param.5), kind=kLoop, calls=%fused_computation.5 | loop fusion | flops 6288384 | bytes 8400896 | tf_op jit(solution)/shard_map/reduce_sum | solution.py:82
  5.4 11.8 %all_to_all.58 = f32[8,1,1024]{2,1,0:T(1,128)S(1)} all-to-all(f32[8,1,1024]{2,1,0:T(1,128)S(1)} %broadcast_in_dim.11), channel_id=1, replica_groups=mesh['row'=16,'col'=8] {'col'}, dimensions={0} | all-to-all | bytes 65536 | tf_op jit(solution)/shard_map/all_to_all | solution.py:19
  18.5 15.6 %all_to_all.59 = f32[16,1,1]{2,1,0:T(1,128)S(1)} all-to-all(f32[16,1,1]{2,1,0:T(1,128)S(1)} %broadcast_in_dim.12), channel_id=1, replica_groups=mesh['row'=16,'col'=8] {'row'}, dimensions={0} | all-to-all | bytes 128 | tf_op jit(solution)/shard_map/all_to_all | solution.py:19
  34.0 0.7 broadcast_in_dim.13
  34.7 4.0 %all-to-all-start.4 = ((f32[16,1,2048]{2,1,0:T(1,128)}), f32[16,1,2048]{2,1,0:T(1,128)S(1)}, u32[]{:S(2)}, u32[]{:S(2)}) async-start(f32[16,1,2048]{2,1,0:T(1,128)} %broadcast_in_dim.13), calls=%async_computation.4 | async-start | bytes 262144 | tf_op jit(solution)/shard_map/all_to_all | solution.py:19
  38.7 7.7 %all-to-all-done.4 = f32[16,1,2048]{2,1,0:T(1,128)S(1)} async-done(((f32[16,1,2048]{2,1,0:T(1,128)}), f32[16,1,2048]{2,1,0:T(1,128)S(1)}, u32[]{:S(2)}, u32[]{:S(2)}) %all-to-all-start.4) | async-done | bytes 131104 | tf_op jit(solution)/shard_map/all_to_all | solution.py:19
  46.4 0.8 broadcast_in_dim.10
  47.3 3.5 %all-to-all-start = ((bf16[8,32,1024]{2,1,0:T(8,128)(2,1)}), bf16[8,32,1024]{2,1,0:T(8,128)(2,1)S(1)}, u32[]{:S(2)}, u32[]{:S(2)}) async-start(bf16[8,32,1024]{2,1,0:T(8,128)(2,1)} %broadcast_in_dim.10), calls=%async_computation | async-start | bytes 1048576 | tf_op jit(solution)/shard_map/all_to_all | solution.py:19
  50.8 9.3 %all-to-all-done = bf16[8,32,1024]{2,1,0:T(8,128)(2,1)S(1)} async-done(((bf16[8,32,1024]{2,1,0:T(8,128)(2,1)}), bf16[8,32,1024]{2,1,0:T(8,128)(2,1)S(1)}, u32[]{:S(2)}, u32[]{:S(2)}) %all-to-all-start) | async-done | bytes 524320 | tf_op jit(solution)/shard_map/all_to_all | solution.py:19
  60.1 1.1 stack.4
  61.2 5.1 %all-to-all-start.1 = ((bf16[16,16,2048]{2,1,0:T(8,128)(2,1)}), bf16[16,16,2048]{2,1,0:T(8,128)(2,1)S(1)}, u32[]{:S(2)}, u32[]{:S(2)}) async-start(bf16[16,16,2048]{2,1,0:T(8,128)(2,1)} %stack.4), calls=%async_computation.1 | async-start | bytes 2097152 | tf_op jit(solution)/shard_map/all_to_all | solution.py:12
  67.7 15.6 %all-to-all-done.1 = bf16[16,16,2048]{2,1,0:T(8,128)(2,1)S(1)} async-done(((bf16[16,16,2048]{2,1,0:T(8,128)(2,1)}), bf16[16,16,2048]{2,1,0:T(8,128)(2,1)S(1)}, u32[]{:S(2)}, u32[]{:S(2)}) %all-to-all-start.1) | async-done | bytes 1048608 | tf_op jit(solution)/shard_map/all_to_all | solution.py:12
  83.4 12.9 %select_convert_fusion.1 = bf16[1024,2048]{1,0:T(8,128)(2,1)S(1)} fusion(s32[1024,2048]{1,0:T(8,128)} %param.5, bf16[256,1024]{1,0:T(8,128)(2,1)S(1)} %bitcast.28, bf16[256,2048]{1,0:T(8,128)(2,1)S(1)} %bitcast.24, f32[2048]{0:T(1024)S(1)} %log.23, f32[1024]{0:T(1024)S(1)} %log.22, f32[]{:T(128)S(6)} %log.21), kind=kOutput, calls=%fused_computation.1 | convolution fusion | flops 1105199104 | bytes 14168068 | tf_op jit(solution)/shard_map/dot_general | solution.py:56
  96.3 2.1 convolution_convert_fusion.3
  98.4 3.6 %all-to-all-start.5 = ((bf16[8,32,1024]{2,1,0:T(8,128)(2,1)}), bf16[8,32,1024]{2,1,0:T(8,128)(2,1)S(1)}, u32[]{:S(2)}, u32[]{:S(2)}) async-start(bf16[8,32,1024]{2,1,0:T(8,128)(2,1)} %bitcast.3), calls=%async_computation.5 | async-start | bytes 1048576 | tf_op jit(solution)/shard_map/all_to_all | solution.py:42
  102.0 4.4 %convolution_convert_fusion = bf16[2048,256]{0,1:T(8,128)(2,1)} fusion(bf16[256,1024]{1,0:T(8,128)(2,1)S(1)} %bitcast.29, bf16[1024,2048]{1,0:T(8,128)(2,1)} %copy-done.5), kind=kOutput, calls=%fused_computation.7 | convolution fusion | flops 1074266112 | bytes 5767168 | tf_op jit(solution)/shard_map/dot_general | solution.py:71
  106.4 4.6 %all-to-all-done.5 = bf16[8,32,1024]{2,1,0:T(8,128)(2,1)S(1)} async-done(((bf16[8,32,1024]{2,1,0:T(8,128)(2,1)}), bf16[8,32,1024]{2,1,0:T(8,128)(2,1)S(1)}, u32[]{:S(2)}, u32[]{:S(2)}) %all-to-all-start.5) | async-done | bytes 524320 | tf_op jit(solution)/shard_map/all_to_all | solution.py:42
  111.1 5.8 %all-to-all-start.6 = ((bf16[16,16,2048]{2,1,0:T(8,128)(2,1)}), bf16[16,16,2048]{2,1,0:T(8,128)(2,1)S(1)}, u32[]{:S(2)}, u32[]{:S(2)}) async-start(bf16[16,16,2048]{2,1,0:T(8,128)(2,1)} %bitcast.5), calls=%async_computation.6 | async-start | bytes 2097152 | tf_op jit(solution)/shard_map/all_to_all | solution.py:42
  117.0 16.8 %all-to-all-done.6 = bf16[16,16,2048]{2,1,0:T(8,128)(2,1)S(1)} async-done(((bf16[16,16,2048]{2,1,0:T(8,128)(2,1)}), bf16[16,16,2048]{2,1,0:T(8,128)(2,1)S(1)}, u32[]{:S(2)}, u32[]{:S(2)}) %all-to-all-start.6) | async-done | bytes 1048608 | tf_op jit(solution)/shard_map/all_to_all | solution.py:42
  133.8 0.8 broadcast_in_dim.14
  134.6 3.5 %all-to-all-start.8 = ((bf16[8,32,1024]{2,1,0:T(8,128)(2,1)}), bf16[8,32,1024]{2,1,0:T(8,128)(2,1)S(1)}, u32[]{:S(2)}, u32[]{:S(2)}) async-start(bf16[8,32,1024]{2,1,0:T(8,128)(2,1)} %broadcast_in_dim.14), calls=%async_computation.8 | async-start | bytes 1048576 | tf_op jit(solution)/shard_map/all_to_all | solution.py:19
  138.3 8.8 %all-to-all-done.8 = bf16[8,32,1024]{2,1,0:T(8,128)(2,1)S(1)} async-done(((bf16[8,32,1024]{2,1,0:T(8,128)(2,1)}), bf16[8,32,1024]{2,1,0:T(8,128)(2,1)S(1)}, u32[]{:S(2)}, u32[]{:S(2)}) %all-to-all-start.8) | async-done | bytes 524320 | tf_op jit(solution)/shard_map/all_to_all | solution.py:19
  147.2 22.6 %all_to_all.60 = bf16[16,16,2048]{2,1,0:T(8,128)(2,1)S(1)} all-to-all(bf16[16,16,2048]{2,1,0:T(8,128)(2,1)S(1)} %stack.5), channel_id=1, replica_groups=mesh['row'=16,'col'=8] {'row'}, dimensions={0} | all-to-all | bytes 2097152 | tf_op jit(solution)/shard_map/all_to_all | solution.py:12
  169.9 12.8 %select_convert_fusion = bf16[1024,2048]{1,0:T(8,128)(2,1)S(1)} fusion(s32[1024,2048]{1,0:T(8,128)} %param.5, bf16[256,1024]{1,0:T(8,128)(2,1)S(1)} %bitcast.30, bf16[256,2048]{1,0:T(8,128)(2,1)S(1)} %bitcast.26, f32[2048]{0:T(1024)S(1)} %log.23, f32[1024]{0:T(1024)S(1)} %log.22, f32[]{:T(128)S(6)} %log.21), kind=kOutput, calls=%fused_computation | convolution fusion | flops 1105199104 | bytes 14168068 | tf_op jit(solution)/shard_map/dot_general | solution.py:56
  182.7 2.1 convolution_convert_fusion.2
  184.8 3.5 %all-to-all-start.9 = ((bf16[8,32,1024]{2,1,0:T(8,128)(2,1)}), bf16[8,32,1024]{2,1,0:T(8,128)(2,1)S(1)}, u32[]{:S(2)}, u32[]{:S(2)}) async-start(bf16[8,32,1024]{2,1,0:T(8,128)(2,1)} %bitcast.8), calls=%async_computation.9 | async-start | bytes 1048576 | tf_op jit(solution)/shard_map/all_to_all | solution.py:42
  188.3 4.4 %convolution_convert_fusion.1 = bf16[256,2048]{1,0:T(8,128)(2,1)} fusion(bf16[256,1024]{1,0:T(8,128)(2,1)S(1)} %bitcast.31, bf16[1024,2048]{1,0:T(8,128)(2,1)} %copy-done.4), kind=kOutput, calls=%fused_computation.8 | convolution fusion | flops 1074266112 | bytes 5767168 | tf_op jit(solution)/shard_map/dot_general | solution.py:71
  192.8 4.4 %all-to-all-done.9 = bf16[8,32,1024]{2,1,0:T(8,128)(2,1)S(1)} async-done(((bf16[8,32,1024]{2,1,0:T(8,128)(2,1)}), bf16[8,32,1024]{2,1,0:T(8,128)(2,1)S(1)}, u32[]{:S(2)}, u32[]{:S(2)}) %all-to-all-start.9) | async-done | bytes 524320 | tf_op jit(solution)/shard_map/all_to_all | solution.py:42
  197.2 5.5 %all-to-all-start.10 = ((bf16[16,16,2048]{2,1,0:T(8,128)(2,1)}), bf16[16,16,2048]{2,1,0:T(8,128)(2,1)S(1)}, u32[]{:S(2)}, u32[]{:S(2)}) async-start(bf16[16,16,2048]{2,1,0:T(8,128)(2,1)} %bitcast.9), calls=%async_computation.10 | async-start | bytes 2097152 | tf_op jit(solution)/shard_map/all_to_all | solution.py:42
  202.8 0.7 multiply_subtract_fusion.1
  203.5 16.3 %all-to-all-done.10 = bf16[16,16,2048]{2,1,0:T(8,128)(2,1)S(1)} async-done(((bf16[16,16,2048]{2,1,0:T(8,128)(2,1)}), bf16[16,16,2048]{2,1,0:T(8,128)(2,1)S(1)}, u32[]{:S(2)}, u32[]{:S(2)}) %all-to-all-start.10) | async-done | bytes 1048608 | tf_op jit(solution)/shard_map/all_to_all | solution.py:42
  220.0 0.7 multiply_subtract_fusion
  (28 shorter events, 2.7 us)
Async XLA Ops:
  0.6 38.1 %copy-start = (f32[32,1024]{1,0:T(8,128)S(1)}, f32[32,1024]{1,0:T(8,128)}, u32[]{:S(2)}) copy-start(f32[32,1024]{1,0:T(8,128)} %param.6) | copy-start | bytes 393220
  0.6 50.1 %copy-start.1 = (f32[16,2048]{1,0:T(8,128)S(1)}, f32[16,2048]{1,0:T(8,128)}, u32[]{:S(2)}) copy-start(f32[16,2048]{1,0:T(8,128)} %param.7) | copy-start | bytes 393220
  34.7 11.7 %all-to-all-start.4 = ((f32[16,1,2048]{2,1,0:T(1,128)}), f32[16,1,2048]{2,1,0:T(1,128)S(1)}, u32[]{:S(2)}, u32[]{:S(2)}) async-start(f32[16,1,2048]{2,1,0:T(1,128)} %broadcast_in_dim.13), calls=%async_computation.4 | async-start | bytes 262144 | tf_op jit(solution)/shard_map/all_to_all | solution.py:19
  47.3 12.9 %all-to-all-start = ((bf16[8,32,1024]{2,1,0:T(8,128)(2,1)}), bf16[8,32,1024]{2,1,0:T(8,128)(2,1)S(1)}, u32[]{:S(2)}, u32[]{:S(2)}) async-start(bf16[8,32,1024]{2,1,0:T(8,128)(2,1)} %broadcast_in_dim.10), calls=%async_computation | async-start | bytes 1048576 | tf_op jit(solution)/shard_map/all_to_all | solution.py:19
  61.2 22.1 %all-to-all-start.1 = ((bf16[16,16,2048]{2,1,0:T(8,128)(2,1)}), bf16[16,16,2048]{2,1,0:T(8,128)(2,1)S(1)}, u32[]{:S(2)}, u32[]{:S(2)}) async-start(bf16[16,16,2048]{2,1,0:T(8,128)(2,1)} %stack.4), calls=%async_computation.1 | async-start | bytes 2097152 | tf_op jit(solution)/shard_map/all_to_all | solution.py:12
  96.2 2.1 copy-start.5
  96.3 20.6 %copy-start.2 = (f32[32,1024]{1,0:T(8,128)S(1)}, f32[32,1024]{1,0:T(8,128)}, u32[]{:S(2)}) copy-start(f32[32,1024]{1,0:T(8,128)} %param.8) | copy-start | bytes 393220
  98.4 39.9 %copy-start.3 = (f32[16,2048]{1,0:T(8,128)S(1)}, f32[16,2048]{1,0:T(8,128)}, u32[]{:S(2)}) copy-start(f32[16,2048]{1,0:T(8,128)} %param.9) | copy-start | bytes 393220
  98.4 12.7 %all-to-all-start.5 = ((bf16[8,32,1024]{2,1,0:T(8,128)(2,1)}), bf16[8,32,1024]{2,1,0:T(8,128)(2,1)S(1)}, u32[]{:S(2)}, u32[]{:S(2)}) async-start(bf16[8,32,1024]{2,1,0:T(8,128)(2,1)} %bitcast.3), calls=%async_computation.5 | async-start | bytes 1048576 | tf_op jit(solution)/shard_map/all_to_all | solution.py:42
  111.1 22.7 %all-to-all-start.6 = ((bf16[16,16,2048]{2,1,0:T(8,128)(2,1)}), bf16[16,16,2048]{2,1,0:T(8,128)(2,1)S(1)}, u32[]{:S(2)}, u32[]{:S(2)}) async-start(bf16[16,16,2048]{2,1,0:T(8,128)(2,1)} %bitcast.5), calls=%async_computation.6 | async-start | bytes 2097152 | tf_op jit(solution)/shard_map/all_to_all | solution.py:42
  134.6 12.5 %all-to-all-start.8 = ((bf16[8,32,1024]{2,1,0:T(8,128)(2,1)}), bf16[8,32,1024]{2,1,0:T(8,128)(2,1)S(1)}, u32[]{:S(2)}, u32[]{:S(2)}) async-start(bf16[8,32,1024]{2,1,0:T(8,128)(2,1)} %broadcast_in_dim.14), calls=%async_computation.8 | async-start | bytes 1048576 | tf_op jit(solution)/shard_map/all_to_all | solution.py:19
  182.7 2.1 copy-start.4
  184.8 12.4 %all-to-all-start.9 = ((bf16[8,32,1024]{2,1,0:T(8,128)(2,1)}), bf16[8,32,1024]{2,1,0:T(8,128)(2,1)S(1)}, u32[]{:S(2)}, u32[]{:S(2)}) async-start(bf16[8,32,1024]{2,1,0:T(8,128)(2,1)} %bitcast.8), calls=%async_computation.9 | async-start | bytes 1048576 | tf_op jit(solution)/shard_map/all_to_all | solution.py:42
  197.2 22.6 %all-to-all-start.10 = ((bf16[16,16,2048]{2,1,0:T(8,128)(2,1)}), bf16[16,16,2048]{2,1,0:T(8,128)(2,1)S(1)}, u32[]{:S(2)}, u32[]{:S(2)}) async-start(bf16[16,16,2048]{2,1,0:T(8,128)(2,1)} %bitcast.9), calls=%async_computation.10 | async-start | bytes 2097152 | tf_op jit(solution)/shard_map/all_to_all | solution.py:42
